TPU v7x, 32 devices: a whole 2x2x4 slice. The times are simulated.
32 devices in a mesh: lat: 4 (over x, core), lon: 8 (over z, y).
Axes of the slice: x: 2, y: 2, z: 4, core: 2. Of those that a mesh axis runs over, the one named last changes fastest.
Arguments:
- features: float32 [16, 256, 1024], P('lat', None, 'lon'), may hold values from -6 to 6
- basis_panels: float32 [16, 3, 9, 255], P('lat'), may hold values from -0.9 to 0.9
- weights: float32 [9, 256, 256], replicated, may hold values from -0.125 to 0.125
- bias_term: float32 [256], replicated, may hold values from -3 to 3
- widths: int32 [16], P('lat'), may hold values from 4 to 127, as said below
- tap_rows: int32 [16, 3], P('lat'), may hold values from -4 to 4, as said below
Outputs:
- convolved: float32 [16, 256, 1024], P('lat', None, 'lon')
Inputs may be any that keep to these rules, and one draw needn't show every extreme that they name: With d = min(i, 15 - i) the distance of row i from the nearer pole, widths[i] is at most min(8 * 16 // (4 * d + 2) + 4, 127), and the first and the last row have the half-width 127. In each aligned block of 4 rows the row nearest a pole has exactly this bound. `tap_rows`: the first row's first tap has the offset -4 and the last row's last tap the offset 4.
All inputs are finite; a program needn't handle non-finite values.
Results may differ from a plain program's by a relative error of at most 0.000062.
Values sent between devices are 32-bit elements; how exact they have to be, the bound alone decides.
No kernel may reach another device: no remote copies, remote signals or barrier semaphores. Data moves between devices by JAX's collectives and lax.ppermute only.
A program may use at most 256 MiB of HBM per device.

v0:
```python
import jax
import jax.numpy as jnp
from jax import lax
from jax.sharding import PartitionSpec as P

REACH = 4


def passed_along(value, axis, by):
    peers = lax.axis_size(axis)
    return lax.ppermute(value, axis, [(i, (i + by) % peers) for i in range(peers)])


def padded_2(block, sides, width):
    for axis, dim in sides:
        count = lax.axis_size(axis)
        forward = [(i, i + 1) for i in range(count - 1)]
        backward = [(target, source) for source, target in forward]
        low = lax.ppermute(
            lax.slice_in_dim(block, block.shape[dim] - width, None, axis=dim), axis, forward
        )
        high = lax.ppermute(lax.slice_in_dim(block, 0, width, axis=dim), axis, backward)
        block = jnp.concatenate([low, block, high], axis=dim)
    return block


def widen(block):
    columns = block.shape[2]
    before = []
    needed = columns - 1
    before.insert(0, passed_along(block[:, :, columns - needed :], "lon", 1))
    after = [passed_along(block[:, :, :needed], "lon", -1)]
    return jnp.concatenate(before + [block] + after, axis=2)


def deepen(block, lon_count):
    padded = padded_2(block, (("lat", 0),), REACH)
    lat_place = lax.axis_index("lat")
    lat_last = lax.axis_size("lat") - 1
    outgoing = jnp.where(lat_place == 0, block, block)
    mirrored = passed_along(outgoing, "lon", lon_count // 2)[::-1]
    upper = jnp.where(lat_place == 0, mirrored, padded[:REACH])
    lower = jnp.where(lat_place == lat_last, mirrored, padded[-REACH:])
    return jnp.concatenate([upper, padded[REACH:-REACH], lower], axis=0)


def per_device(features, basis_panels, weights, bias_term, widths, tap_rows):
    row_count, channels, columns = features.shape
    lon_count = lax.axis_size("lon")
    hop_count = min(1, lon_count // 2)
    half_width = hop_count * columns - 1
    extended = widen(deepen(features, lon_count))
    window = extended.shape[2]
    lag_table = (
        jnp.arange(window, dtype=jnp.int32)[:, None] - jnp.arange(columns, dtype=jnp.int32)[None, :]
    )
    clipped = jnp.clip(lag_table, 0, 2 * half_width)
    in_panel = (lag_table >= 0) & (lag_table <= 2 * half_width)

    def one_row(row_index):
        reach_limit = widths[row_index]
        inside_band = in_panel & (jnp.abs(lag_table - half_width) <= reach_limit)
        gathered_panel = jnp.take(basis_panels[row_index], clipped, axis=2)
        toeplitz = jnp.where(inside_band[None, None], gathered_panel, jnp.zeros((), jnp.float32))
        chosen = jnp.take(extended, row_index + REACH + tap_rows[row_index], axis=0)
        correlated = jnp.einsum("tcm,tkml->kcl", chosen, toeplitz, precision=lax.Precision.HIGHEST)
        mixed = jnp.einsum("koc,kcl->ol", weights, correlated, precision=lax.Precision.HIGHEST)
        return mixed + bias_term[:, None]

    return lax.map(one_row, jnp.arange(row_count, dtype=jnp.int32))


def solution(mesh):
    return jax.shard_map(
        per_device,
        mesh=mesh,
        in_specs=(
            P("lat", None, "lon"),
            P("lat", None, None, None),
            P(),
            P(),
            P("lat"),
            P("lat", None),
        ),
        out_specs=P("lat", None, "lon"),
        check_vma=False,
    )
```

profile of v0, /device:TPU:0, one launch (start us, length us, event | category | flops | bytes accessed | tf_op | source)
XLA Modules:
  0.0 1400.8 jit_solution(11147549616724298228)
XLA Ops:
  0.0 2.6 collective-permute-start.1
  2.6 3.5 collective-permute-start
  7.3 21.8 %collective-permute-done = f32[4,256,128]{2,1,0:T(8,128)S(1)} collective-permute-done((f32[4,256,128]{2,1,0:T(8,128)}, f32[4,256,128]{2,1,0:T(8,128)S(1)}, u32[]{:S(2)}, u32[]{:S(2)}) %collective-permute-start) | collective-permute-done | bytes 524320 | tf_op jit(solution)/shard_map/ppermute | solution.py:11
  31.6 5.8 collective-permute-start.4
  37.4 65.5 %collective-permute-done.4 = f32[12,256,127]{2,1,0:T(8,128)} collective-permute-done((f32[12,256,127]{2,1,0:T(8,128)}, f32[12,256,127]{2,1,0:T(8,128)}, u32[]{:S(2)}, u32[]{:S(2)}) %collective-permute-start.4) | collective-permute-done | bytes 1560608 | tf_op jit(solution)/shard_map/ppermute | solution.py:11
  103.1 5.6 pad_maximum_fusion
  109.3 1291.5 %while.14 = (s32[]{:T(128)}, f32[4,256,128]{2,1,0:T(8,128)}, s32[4]{0:T(128)}, s32[4]{0:T(128)S(1)}, f32[4,3,9,255]{3,0,2,1:T(4,128)}, /*index=5*/s32[4,3]{1,0:T...) while((s32[]{:T(128)}, f32[4,256,128]{2,1,0:T(8,128)}, ...), condition=%wide.region_1.2_spmd.clone.clone, body=%wide.region_0.1_spmd.clone.clone.sunk | while | flops 4965594112 | bytes 36392804 | solution.py:70
  113.6 243.8 %gather_fusion = f32[48896,3,9]{2,1,0:T(4,128)} fusion(f32[3,9,255]{1,0,2:T(4,128)S(1)} %bitcast.72, s32[49152]{0:T(1024)S(1)} %pad_clamp_fusion.4), kind=kCustom, calls=%fused_computation.clone.clone.1 | custom fusion | bytes 10757120 | tf_op jit(solution)/shard_map/while/body/eval_jaxpr/jit(_take)/gather | solution.py:63
  357.4 55.2 %copy.22 = f32[382,128,3,9]{1,0,2,3:T(8,128)} copy(f32[382,128,3,9]{3,2,1,0:T(4,128)} %bitcast.70) | data formatting | bytes 10561536 | tf_op jit(solution)/shard_map/while/body/eval_jaxpr/jit(_take)/gather | solution.py:63
  414.7 3.0 gather_fusion.1
  417.7 11.3 fusion.58
  436.4 243.8 %gather_fusion = f32[48896,3,9]{2,1,0:T(4,128)} fusion(f32[3,9,255]{1,0,2:T(4,128)S(1)} %bitcast.72, s32[49152]{0:T(1024)S(1)} %pad_clamp_fusion.4), kind=kCustom, calls=%fused_computation.clone.clone.1 | custom fusion | bytes 10757120 | tf_op jit(solution)/shard_map/while/body/eval_jaxpr/jit(_take)/gather | solution.py:63
  680.3 55.2 %copy.22 = f32[382,128,3,9]{1,0,2,3:T(8,128)} copy(f32[382,128,3,9]{3,2,1,0:T(4,128)} %bitcast.70) | data formatting | bytes 10561536 | tf_op jit(solution)/shard_map/while/body/eval_jaxpr/jit(_take)/gather | solution.py:63
  737.6 3.0 gather_fusion.1
  740.5 11.3 fusion.58
  751.9 2.5 fusion.59
  759.3 243.8 %gather_fusion = f32[48896,3,9]{2,1,0:T(4,128)} fusion(f32[3,9,255]{1,0,2:T(4,128)S(1)} %bitcast.72, s32[49152]{0:T(1024)S(1)} %pad_clamp_fusion.4), kind=kCustom, calls=%fused_computation.clone.clone.1 | custom fusion | bytes 10757120 | tf_op jit(solution)/shard_map/while/body/eval_jaxpr/jit(_take)/gather | solution.py:63
  1003.1 55.2 %copy.22 = f32[382,128,3,9]{1,0,2,3:T(8,128)} copy(f32[382,128,3,9]{3,2,1,0:T(4,128)} %bitcast.70) | data formatting | bytes 10561536 | tf_op jit(solution)/shard_map/while/body/eval_jaxpr/jit(_take)/gather | solution.py:63
  1060.4 3.0 gather_fusion.1
  1063.4 11.3 fusion.58
  1082.1 243.8 %gather_fusion = f32[48896,3,9]{2,1,0:T(4,128)} fusion(f32[3,9,255]{1,0,2:T(4,128)S(1)} %bitcast.72, s32[49152]{0:T(1024)S(1)} %pad_clamp_fusion.4), kind=kCustom, calls=%fused_computation.clone.clone.1 | custom fusion | bytes 10757120 | tf_op jit(solution)/shard_map/while/body/eval_jaxpr/jit(_take)/gather | solution.py:63
  1325.9 55.2 %copy.22 = f32[382,128,3,9]{1,0,2,3:T(8,128)} copy(f32[382,128,3,9]{3,2,1,0:T(4,128)} %bitcast.70) | data formatting | bytes 10561536 | tf_op jit(solution)/shard_map/while/body/eval_jaxpr/jit(_take)/gather | solution.py:63
  1383.2 3.0 gather_fusion.1
  1386.2 11.3 fusion.58
  (71 shorter events, 33.1 us)
Async XLA Ops:
  0.0 29.3 %copy-start.1 = (f32[4,256,128]{2,1,0:T(8,128)S(1)}, f32[4,256,128]{2,1,0:T(8,128)}, u32[]{:S(2)}) copy-start(f32[4,256,128]{2,1,0:T(8,128)} %param.8) | copy-start | bytes 1572868
  0.0 7.3 collective-permute-start.1
  2.6 26.6 %collective-permute-start = (f32[4,256,128]{2,1,0:T(8,128)}, f32[4,256,128]{2,1,0:T(8,128)S(1)}, u32[]{:S(2)}, u32[]{:S(2)}) collective-permute-start(f32[4,256,128]{2,1,0:T(8,128)} %param.8), channel_id=1, source_target_pairs={{0,4},{1,5},{2,6},{3,7},{4,0},{5,1},{6,2},{7,3},{8,12},{9,13},{10,... | collective-permute-start | bytes 1572872 | tf_op jit(solution)/shard_map/ppermute | solution.py:11
  6.0 23.1 %collective-permute-start.2 = (f32[4,256,128]{2,1,0:T(8,128)}, f32[4,256,128]{2,1,0:T(8,128)S(1)}, u32[]{:S(2)}, u32[]{:S(2)}) collective-permute-start(f32[4,256,128]{2,1,0:T(8,128)} %param.8), channel_id=1, source_target_pairs={{8,0},{16,8},{24,16},{9,1},{17,9},{25,17},{10,2},{18,10},{26,18},{... | collective-permute-start | bytes 1572872 | tf_op jit(solution)/shard_map/ppermute | solution.py:22
  31.6 71.3 %collective-permute-start.4 = (f32[12,256,127]{2,1,0:T(8,128)}, f32[12,256,127]{2,1,0:T(8,128)}, u32[]{:S(2)}, u32[]{:S(2)}) collective-permute-start(f32[12,256,127]{2,1,0:T(8,128)} %get-tuple-element.238), channel_id=1, source_target_pairs={{0,7},{1,0},{2,1},{3,2},{4,3},{5,4},{6,5},{7,6},{8,15},{9,8},{10,9... | collective-permute-start | bytes 4681736 | tf_op jit(solution)/shard_map/ppermute | solution.py:11
  37.4 65.7 %collective-permute-start.3 = (f32[12,256,127]{2,1,0:T(8,128)}, f32[12,256,127]{2,1,0:T(8,128)}, u32[]{:S(2)}, u32[]{:S(2)}) collective-permute-start(f32[12,256,127]{2,1,0:T(8,128)} %get-tuple-element.237), channel_id=1, source_target_pairs={{0,1},{1,2},{2,3},{3,4},{4,5},{5,6},{6,7},{7,0},{8,9},{9,10},{10,1... | collective-permute-start | bytes 4681736 | tf_op jit(solution)/shard_map/ppermute | solution.py:11
  37.4 71.9 %copy-start = (f32[9,256,256]{2,1,0:T(8,128)S(1)}, f32[9,256,256]{2,1,0:T(8,128)}, u32[]{:S(2)}) copy-start(f32[9,256,256]{2,1,0:T(8,128)} %param.10) | copy-start | bytes 7077892
  37.4 71.9 %copy-start.2 = (f32[256]{0:T(256)S(1)}, f32[256]{0:T(256)}, u32[]{:S(2)}) copy-start(f32[256]{0:T(256)} %param.11) | copy-start | bytes 3076
  37.4 71.9 %copy-start.3 = (s32[4,3]{1,0:T(4,128)S(1)}, s32[4,3]{1,0:T(4,128)}, u32[]{:S(2)}) copy-start(s32[4,3]{1,0:T(4,128)} %param.13) | copy-start | bytes 148
  37.4 71.8 %copy-start.4 = (s32[4]{0:T(128)S(1)}, s32[4]{0:T(128)}, u32[]{:S(2)}) copy-start(s32[4]{0:T(128)} %param.12) | copy-start | bytes 52
where the time goes:
time: 1400 us
  local copies, waits for them, and re-layouts  1230 us (88%)
  waiting for transfers between devices  87.5 us (6%)
  matrix products  55.1 us (4%)
    gather x8, local copies, waits for them, and re-layouts, one_row(): gathered_panel = jnp.take(basis_panels[row_index], clipped, axis=2)  1200 us
    ppermute x3, waiting for transfers between devices, passed_along(): lax.ppermute(value, axis, [(i, (i + by) % peers) for i in range(peers)])  87.5 us
    dot_general x4, matrix products, one_row(): jnp.einsum('tcm,tkml->kcl', chosen, toeplitz, precision=lax.Precision.HIG...  45.2 us
  transfers between devices with their start and end apart: 5, of which 3 were waited for; matrix products, arithmetic and copies ran while one was open for 0% of the time, Pallas kernels for 0%

commit v1 on v0

v1 whole, which is shorter than its diff:
```python
import functools

import jax
import jax.numpy as jnp
import numpy as np
from jax import lax
from jax.experimental import pallas as pl
from jax.experimental.pallas import tpu as pltpu
from jax.sharding import PartitionSpec as P

REACH = 4
TILE = 16
VMEM = pl.BlockSpec(memory_space=pltpu.VMEM)
SMEM = pl.BlockSpec(memory_space=pltpu.SMEM)
CONTRACT_LAST = (((1,), (1,)), ((), ()))


def shifted(value, axis, by):
    peers = lax.axis_size(axis)
    return lax.ppermute(value, axis, [(i, (i + by) % peers) for i in range(peers)])


def slot_reach(lat_count, rows, half_width):
    total = lat_count * rows
    reach = [0] * rows
    for block in range(lat_count):
        order = range(rows) if 2 * block < lat_count else reversed(range(rows))
        for slot, row in enumerate(order):
            place = block * rows + row
            distance = min(place, total - 1 - place)
            bound = min(8 * total // (4 * distance + 2) + 4, half_width)
            reach[slot] = max(reach[slot], half_width if distance == 0 else bound)
    return [-(-bound // TILE) * TILE for bound in reach]


def halves(value):
    high = value.astype(jnp.bfloat16)
    return high, (value - high.astype(jnp.float32)).astype(jnp.bfloat16)


def dot_last(left, right):
    return lax.dot_general(left, right, CONTRACT_LAST, preferred_element_type=jnp.float32)


def bands_kernel(reach, taps, half, panel_ref, weight_ref, centre_ref, *rest):
    edge_refs, (high_ref, low_ref) = rest[: len(reach)], rest[len(reach) :]
    columns = centre_ref.shape[2]

    def put(out_ref, where, chunk, first, count, tap):
        spread = jnp.broadcast_to(chunk, (count, 2 * columns))
        turned = pltpu.roll(
            spread, 2 * columns - half + first, axis=1, stride=1, stride_axis=0
        )[:, :columns]
        high, low = halves(turned)
        out_ref[where + (slice(tap * columns, (tap + 1) * columns),)] = high
        out_ref[where + (slice((taps + tap) * columns, (taps + tap + 1) * columns),)] = low

    for slot, width in enumerate(reach):
        for tap in range(taps):
            row = panel_ref[0, slot * taps + tap : slot * taps + tap + 1, :]
            put(centre_ref, (slot, 0, slice(None)), row[:, columns : 3 * columns], 0, columns, tap)
            edge = edge_refs[slot]
            put(edge, (0, slice(0, width)), row[:, 2 * columns :], columns - width, width, tap)
            put(edge, (0, slice(width, 2 * width)), row[:, : 2 * columns], 0, width, tap)
    high, low = halves(weight_ref[0])
    high_ref[...] = high
    low_ref[...] = low


def mixed(scratch_ref, high_ref, low_ref):
    depth = high_ref.shape[1]
    upper = scratch_ref[:, :depth]
    total = dot_last(upper, high_ref[...])
    total += dot_last(scratch_ref[:, depth:], high_ref[...])
    return total + dot_last(upper, low_ref[...])


def correlate(band_ref, spread_ref, low_ref, slot, put):
    basis, lines, depth = band_ref.shape
    band = band_ref[...].reshape(basis * lines, depth)
    total = dot_last(band, spread_ref[slot]) + dot_last(band[:, : depth // 2], low_ref[slot])
    high, low = halves(total)
    for k in range(basis):
        put(k, high[k * lines : (k + 1) * lines], low[k * lines : (k + 1) * lines])


def edges_kernel(reach, taps, code_ref, own, above, below, turned, *rest):
    edge_refs = rest[: len(reach)]
    high_ref, low_ref, left_ref, right_ref, spread_ref, rest_ref, scratch = rest[len(reach) :]
    columns = own.shape[2]
    channels = own.shape[1]
    depth = high_ref.shape[1]

    for slot in range(len(reach)):
        for tap in range(taps):
            at = slot * taps + tap

            def put(source, at=at, slot=slot, tap=tap):
                high, low = halves(source[code_ref[1, at]])
                spread_ref[slot, :, tap * columns : (tap + 1) * columns] = high
                spread_ref[slot, :, (taps + tap) * columns : (taps + tap + 1) * columns] = high
                rest_ref[slot, :, tap * columns : (tap + 1) * columns] = low

            for number, source in enumerate((own, above, below, turned)):
                pl.when(code_ref[0, at] == number)(functools.partial(put, source))

    total = sum(reach)
    start = 0
    for slot, width in enumerate(reach):

        def keep(k, high, low, start=start, width=width):
            lanes = slice(k * channels, (k + 1) * channels)
            lower = slice(depth + k * channels, depth + (k + 1) * channels)
            scratch[start : start + width, lanes] = high[:width]
            scratch[start : start + width, lower] = low[:width]
            scratch[total + start : total + start + width, lanes] = high[width:]
            scratch[total + start : total + start + width, lower] = low[width:]

        correlate(edge_refs[slot], spread_ref, rest_ref, slot, keep)
        start += width
    result = mixed(scratch, high_ref, low_ref)
    left_ref[...] = result[:total]
    right_ref[...] = result[total:]


def centre_kernel(spread_ref, rest_ref, band_ref, high_ref, low_ref, out_ref, scratch):
    rows, _, columns, _ = band_ref.shape
    channels = spread_ref.shape[1]
    depth = high_ref.shape[1]
    for slot in range(rows):

        def keep(k, high, low, slot=slot):
            lines = slice(slot * columns, (slot + 1) * columns)
            scratch[lines, k * channels : (k + 1) * channels] = high
            scratch[lines, depth + k * channels : depth + (k + 1) * channels] = low

        correlate(band_ref.at[slot], spread_ref, rest_ref, slot, keep)
    out_ref[...] = mixed(scratch, high_ref, low_ref).reshape(out_ref.shape)


def join_kernel(reach, order_ref, centre_ref, east_ref, west_ref, bias_ref, out_ref):
    columns = out_ref.shape[2]
    start = 0
    for slot, width in enumerate(reach):
        part = centre_ref[slot] + bias_ref[...]
        east = east_ref[start : start + width]
        west = west_ref[start : start + width]
        if width < columns:
            gap = jnp.zeros((columns - width, part.shape[1]), jnp.float32)
            east = jnp.concatenate([gap, east], axis=0)
            west = jnp.concatenate([west, gap], axis=0)
        out_ref[order_ref[slot]] = (part + east + west).T
        start += width


def per_device(features, basis_panels, weights, bias_term, widths, tap_rows):
    rows, channels, columns = features.shape
    _, taps, basis, span = basis_panels.shape
    outs = weights.shape[1]
    half = (span - 1) // 2
    lat_count, lon_count = lax.axis_size("lat"), lax.axis_size("lon")
    place, last = lax.axis_index("lat"), lat_count - 1
    reach = slot_reach(lat_count, rows, half)

    polar = [
        (block * lon_count + at, block * lon_count + (at + lon_count // 2) % lon_count)
        for block in sorted({0, last})
        for at in range(lon_count)
    ]
    turned = lax.ppermute(features, ("lat", "lon"), polar)
    above = lax.ppermute(features, "lat", [(i, i + 1) for i in range(last)])
    below = lax.ppermute(features, "lat", [(i + 1, i) for i in range(last)])

    slots = jnp.arange(rows, dtype=jnp.int32)
    order = jnp.where(2 * place < lat_count, slots, rows - 1 - slots)
    line = order[:, None] + jnp.where(2 * place < lat_count, tap_rows, tap_rows[::-1])
    line = line.reshape(-1)
    up, down = line < 0, line >= rows
    source = jnp.where(
        up,
        jnp.where(place == 0, 3, 1),
        jnp.where(down, jnp.where(place == last, 3, 2), 0),
    )
    row = jnp.where(
        up,
        jnp.where(place == 0, -1 - line, rows + line),
        jnp.where(down, jnp.where(place == last, 2 * rows - 1 - line, line - rows), line),
    )
    codes = jnp.stack([source, row]).astype(jnp.int32)

    offsets = jnp.abs(jnp.arange(span, dtype=jnp.int32) - half)
    masked = jnp.where(offsets <= widths[:, None, None, None], basis_panels, 0.0)
    masked = jnp.where(2 * place < lat_count, masked, masked[::-1])
    masked = jnp.pad(masked, ((0, 0),) * 3 + ((columns, 3 * columns - span),))
    panels = masked.transpose(2, 0, 1, 3).reshape(basis, rows * taps, 4 * columns)

    bands = pl.pallas_call(
        functools.partial(bands_kernel, reach, taps, half),
        grid=(basis,),
        in_specs=[
            pl.BlockSpec((1, rows * taps, 4 * columns), lambda k: (k, 0, 0)),
            pl.BlockSpec((1, outs, channels), lambda k: (k, 0, 0)),
        ],
        out_specs=[pl.BlockSpec((rows, 1, columns, 2 * taps * columns), lambda k: (0, k, 0, 0))]
        + [
            pl.BlockSpec((1, 2 * width, 2 * taps * columns), lambda k: (k, 0, 0))
            for width in reach
        ]
        + [pl.BlockSpec((outs, channels), lambda k: (0, k))] * 2,
        out_shape=[
            jax.ShapeDtypeStruct((rows, basis, columns, 2 * taps * columns), jnp.bfloat16)
        ]
        + [
            jax.ShapeDtypeStruct((basis, 2 * width, 2 * taps * columns), jnp.bfloat16)
            for width in reach
        ]
        + [jax.ShapeDtypeStruct((outs, basis * channels), jnp.bfloat16)] * 2,
        name="bands",
    )(panels, weights)
    centre_band, edge_bands, (high, low) = bands[0], bands[1 : rows + 1], bands[rows + 1 :]

    edge = jax.ShapeDtypeStruct((sum(reach), outs), jnp.float32)
    to_west, to_east, spread, spread_low = pl.pallas_call(
        functools.partial(edges_kernel, reach, taps),
        in_specs=[SMEM] + [VMEM] * (6 + rows),
        out_specs=[VMEM] * 4,
        out_shape=[
            edge,
            edge,
            jax.ShapeDtypeStruct((rows, channels, 2 * taps * columns), jnp.bfloat16),
            jax.ShapeDtypeStruct((rows, channels, taps * columns), jnp.bfloat16),
        ],
        scratch_shapes=[pltpu.VMEM((2 * sum(reach), 2 * basis * channels), jnp.bfloat16)],
        name="edges",
    )(codes, features, above, below, turned, *edge_bands, high, low)

    from_east = shifted(to_west, "lon", -1)
    from_west = shifted(to_east, "lon", 1)

    centre = pl.pallas_call(
        centre_kernel,
        in_specs=[VMEM] * 5,
        out_specs=VMEM,
        out_shape=jax.ShapeDtypeStruct((rows, columns, outs), jnp.float32),
        scratch_shapes=[pltpu.VMEM((rows * columns, 2 * basis * channels), jnp.bfloat16)],
        name="centre",
    )(spread, spread_low, centre_band, high, low)

    return pl.pallas_call(
        functools.partial(join_kernel, reach),
        in_specs=[SMEM] + [VMEM] * 4,
        out_specs=VMEM,
        out_shape=jax.ShapeDtypeStruct((rows, outs, columns), jnp.float32),
        name="join",
    )(order, centre, from_east, from_west, bias_term[None, :])


def solution(mesh):
    return jax.shard_map(
        per_device,
        mesh=mesh,
        in_specs=(
            P("lat", None, "lon"),
            P("lat", None, None, None),
            P(),
            P(),
            P("lat"),
            P("lat", None),
        ),
        out_specs=P("lat", None, "lon"),
        check_vma=False,
    )
```

time: 1400 us -> 60 us (0.04)
  local copies, waits for them, and re-layouts: 1230 us -> 3.83 us
  waiting for transfers between devices: 87.5 us -> 0.01 us
  matrix products: 55.1 us -> 0 us
  Pallas kernels: 0 us -> 38.9 us
    gather x12 -> x0, local copies, waits for them, and re-layouts: 1210 us -> none  [the longest x8 1200 us: one_row(): gathered_panel = jnp.take(basis_panels[row_index], clipped, axis=2)]
    ppermute x5, waiting for transfers between devices: 87.5 us -> 0.01 us  [the longest x2 0.01 us: shifted(): lax.ppermute(value, axis, [(i, (i + by) % peers) for i in range(peers)])]
    dot_general x8 -> x0, matrix products: 55.1 us -> none  [the longest x4 45.2 us: one_row(): jnp.einsum('tcm,tkml->kcl', chosen, toeplitz, precision=lax.Precision.HIG...]
    pallas_call x0 -> x4, Pallas kernels: none -> 38.9 us  [the longest x1 13.6 us: per_device(): pl.pallas_call(centre_kernel, in_specs=[VMEM] * 5, out_specs=VMEM, out_sh...]
  transfers between devices with their start and end apart: 5 -> 5, of which waited for: 3 -> 0; matrix products, arithmetic and copies ran while one was open for 0% -> 10% of each run, Pallas kernels for 0% -> 41%
where the time goes in v1:
time: 60 us; the launch traced here: 59.5 us
  Pallas kernels  38.9 us (65%)
  starting transfers between devices  12.6 us (21%)
  other arithmetic  3.95 us (7%)
  local copies, waits for them, and re-layouts  3.83 us (6%)
    pallas_call x1, Pallas kernels, per_device(): pl.pallas_call(centre_kernel, in_specs=[VMEM] * 5, out_specs=VMEM, out_sh...  13.6 us
    pallas_call x1, Pallas kernels, per_device(): pl.pallas_call(functools.partial(edges_kernel, reach, taps), in_specs=[SM...  12.3 us
    pallas_call x1, Pallas kernels, per_device(): pl.pallas_call(functools.partial(bands_kernel, reach, taps, half), grid=(...  10.8 us
    ppermute x1, starting transfers between devices, per_device(): turned = lax.ppermute(features, ('lat', 'lon'), polar)  5.98 us
    ppermute x1, starting transfers between devices, per_device(): above = lax.ppermute(features, 'lat', [(i, i + 1) for i in range(last)])  3.07 us
    ppermute x2, starting transfers between devices, shifted(): lax.ppermute(value, axis, [(i, (i + by) % peers) for i in range(peers)])  2.31 us
    pallas_call x1, Pallas kernels, per_device(): pl.pallas_call(functools.partial(join_kernel, reach), in_specs=[SMEM] + [...  2.2 us
    unnamed x12, local copies, waits for them, and re-layouts  1.86 us
  transfers between devices with their start and end apart: 5, of which 0 were waited for; matrix products, arithmetic and copies ran while one was open for 10% of the time, Pallas kernels for 41%

profile of v1, /device:TPU:0, one launch (start us, length us, event | category | flops | bytes accessed | tf_op | source)
XLA Modules:
  0.0 59.5 jit_solution(3483870929161519979)
XLA Ops:
  0.0 1.3 %collective-permute-start.1 = (f32[4,256,128]{2,1,0:T(8,128)}, f32[4,256,128]{2,1,0:T(8,128)S(1)}, u32[]{:S(2)}, u32[]{:S(2)}) collective-permute-start(f32[4,256,128]{2,1,0:T(8,128)} %own.1), channel_id=1, source_target_pairs={{8,0},{16,8},{24,16},{9,1},{17,9},{25,17},{10,2},{18,10},{26,18},{... | collective-permute-start | bytes 1572872 | tf_op jit(solution)/shard_map/ppermute | solution.py:172
  1.3 3.1 %collective-permute-start = (f32[4,256,128]{2,1,0:T(8,128)}, f32[4,256,128]{2,1,0:T(8,128)S(1)}, u32[]{:S(2)}, u32[]{:S(2)}) collective-permute-start(f32[4,256,128]{2,1,0:T(8,128)} %own.1), channel_id=1, source_target_pairs={{0,8},{8,16},{16,24},{1,9},{9,17},{17,25},{2,10},{10,18},{18,26},{... | collective-permute-start | bytes 1572872 | tf_op jit(solution)/shard_map/ppermute | solution.py:171
  4.4 6.0 %collective-permute-start.2 = (f32[4,256,128]{2,1,0:T(8,128)}, f32[4,256,128]{2,1,0:T(8,128)S(1)}, u32[]{:S(2)}, u32[]{:S(2)}) collective-permute-start(f32[4,256,128]{2,1,0:T(8,128)} %own.1), channel_id=1, source_target_pairs={{0,4},{1,5},{2,6},{3,7},{4,0},{5,1},{6,2},{7,3},{24,28},{25,29},{2... | collective-permute-start | bytes 1572872 | tf_op jit(solution)/shard_map/ppermute | solution.py:170
  10.4 0.7 %rev.6 = s32[4,3]{1,0:T(4,128)S(1)} reverse(s32[4,3]{1,0:T(4,128)} %param.11), dimensions={0} | reverse | bytes 96 | tf_op jit(solution)/shard_map/rev | solution.py:176
  11.1 0.7 %broadcast_compare_fusion = pred[4,255]{1,0:T(4,128)(4,1)S(1)} fusion(s32[255]{0:T(256)S(1)} %add_abs_fusion, s32[4]{0:T(128)} %param.10), kind=kLoop, calls=%fused_computation.5 | loop fusion | flops 1020 | bytes 2056 | tf_op jit(solution)/shard_map/le | solution.py:192
  11.8 0.9 %broadcast_select_fusion = f32[4,3,9,255]{3,0,2,1:T(4,128)S(1)} fusion(f32[4,3,9,255]{3,0,2,1:T(4,128)} %param.7, pred[4,255]{1,0:T(4,128)(4,1)S(1)} %broadcast_compare_fusion), kind=kLoop, calls=%fused_computation.1 | loop fusion | flops 27540 | bytes 221340 | tf_op jit(solution)/shard_map/jit(_where)/select_n | solution.py:192
  12.7 0.2 rev.7
  13.0 0.9 %broadcast_select_fusion.1 = f32[4,3,9,255]{3,0,2,1:T(4,128)S(1)} fusion(f32[4,3,9,255]{3,0,2,1:T(4,128)S(1)} %rev.7, pred[]{:T(512)S(6)} %lt.19, f32[4,3,9,255]{3,0,2,1:T(4,128)} %param.7, pred[4,255]{1,0:T(4,128)(4,1)S(1)} %broadcast_compare_fusion), kind=kLoop, calls=%fused_computation.2 | loop fusion | flops 55080 | bytes 331501 | tf_op jit(solution)/shard_map/jit(_where)/select_n | solution.py:193
  13.9 0.8 %select_add_fusion = s32[4,3]{1,0:T(4,128)S(1)} fusion(s32[4,3]{1,0:T(4,128)} %param.11, s32[4,3]{1,0:T(4,128)S(1)} %rev.6, s32[4]{0:T(128)S(1)} %broadcast_select_fusion.4.order_ref, pred[]{:T(512)S(6)} %lt.19), kind=kLoop, calls=%fused_computation.6 | loop fusion | flops 24 | bytes 161 | tf_op jit(solution)/shard_map/add | solution.py:176
  14.7 0.1 reshape.132
  14.8 0.1 copy.8
  14.9 0.8 %reshape.133.panel_ref = f32[9,12,512]{2,1,0:T(8,128)} reshape(f32[9,4,3,512]{3,2,1,0:T(4,128)S(1)} %copy.8) | data formatting | bytes 442368 | tf_op jit(solution)/shard_map/reshape | solution.py:195
  15.7 10.8 %bands.1 = (bf16[4,9,128,768]{3,2,1,0:T(8,128)(2,1)}, bf16[9,256,768]{2,1,0:T(8,128)(2,1)}, bf16[9,64,768]{2,1,0:T(8,128)(2,1)}, bf16[9,32,768]{2,1,0:T(8,128)(2...) custom-call(f32[9,12,512]{2,1,0:T(8,128)} %reshape.133.panel_ref, ...), custom_call_target="tpu_custom_call" | custom-call | tf_op jit(solution)/shard_map/bands/pallas_call | solution.py:197
  26.6 0.6 pad_add_fusion.code_ref
  27.2 0.0 copy-start.1
  27.2 0.8 %copy-done = f32[4,256,128]{2,1,0:T(8,128)} copy-done((f32[4,256,128]{2,1,0:T(8,128)}, f32[4,256,128]{2,1,0:T(8,128)S(1)}, u32[]{:S(2)}) %copy-start) | copy-done | bytes 524312
  28.0 0.2 copy-done.1
  28.2 0.2 copy-done.2
  28.3 12.3 %edges.1 = (f32[192,256]{1,0:T(8,128)}, f32[192,256]{1,0:T(8,128)}, bf16[4,256,768]{2,1,0:T(8,128)(2,1)}, bf16[4,256,384]{2,1,0:T(8,128)(2,1)}) custom-call(s32[2,12]{1,0:T(2,128)} %pad_add_fusion.code_ref, f32[4,256,128]{2,1,0:T(8,128)} %own.1, f32[4,256,128]{2,1,0:T(8,128)} %copy-done.1, f32[4,256,128]{2,1,0:T(8,128)} %copy-done, ...), custom_call_target="tpu_custom_call" | custom-call | tf_op jit(solution)/shard_map/edges/pallas_call | solution.py:223
  40.6 2.3 %collective-permute-start.3 = (f32[192,256]{1,0:T(8,128)}, f32[192,256]{1,0:T(8,128)S(1)}, u32[]{:S(2)}, u32[]{:S(2)}) collective-permute-start(f32[192,256]{1,0:T(8,128)} %get-tuple-element.25), channel_id=1, source_target_pairs={{0,7},{1,0},{2,1},{3,2},{4,3},{5,4},{6,5},{7,6},{8,15},{9,8},{10,9... | collective-permute-start | bytes 589832 | tf_op jit(solution)/shard_map/ppermute | solution.py:20
  42.9 13.6 %centre.1.centre_ref = f32[4,128,256]{2,1,0:T(8,128)} custom-call(bf16[4,256,768]{2,1,0:T(8,128)(2,1)} %get-tuple-element.22.spread_ref, bf16[4,256,384]{2,1,0:T(8,128)(2,1)} %get-tuple-element.23.rest_ref, bf16[4,9,128,768]{3,2,1,0:T(8,128)(2,1)} %get-tuple-element.24.band_ref, bf16[256,2304]{1,0:T(8,128)(2,1)} %get-tuple-element.20.rest_4_.high_ref, ...), custom_call_target="tpu_custom_call" | custom-call | tf_op jit(solution)/shard_map/centre/pallas_call | solution.py:240
  56.6 0.7 %copy-done.3 = f32[192,256]{1,0:T(8,128)} copy-done((f32[192,256]{1,0:T(8,128)}, f32[192,256]{1,0:T(8,128)S(1)}, u32[]{:S(2)}) %copy-start.3) | copy-done | bytes 196632
  57.2 0.1 copy-done.4
  57.3 2.2 %join.1 = f32[4,256,128]{2,1,0:T(8,128)} custom-call(s32[4]{0:T(128)} %copy-done.5, f32[4,128,256]{2,1,0:T(8,128)} %centre.1.centre_ref, f32[192,256]{1,0:T(8,128)} %copy-done.3, f32[192,256]{1,0:T(8,128)} %copy-done.4, f32[1,256]{1,0:T(1,128)} %bitcast.3), custom_call_target="tpu_custom_call" | custom-call | tf_op jit(solution)/shard_map/join/pallas_call | solution.py:249
  (16 shorter events, 0.1 us)
Async XLA Ops:
  0.0 27.2 %collective-permute-start.1 = (f32[4,256,128]{2,1,0:T(8,128)}, f32[4,256,128]{2,1,0:T(8,128)S(1)}, u32[]{:S(2)}, u32[]{:S(2)}) collective-permute-start(f32[4,256,128]{2,1,0:T(8,128)} %own.1), channel_id=1, source_target_pairs={{8,0},{16,8},{24,16},{9,1},{17,9},{25,17},{10,2},{18,10},{26,18},{... | collective-permute-start | bytes 1572872 | tf_op jit(solution)/shard_map/ppermute | solution.py:172
  1.3 25.9 %collective-permute-start = (f32[4,256,128]{2,1,0:T(8,128)}, f32[4,256,128]{2,1,0:T(8,128)S(1)}, u32[]{:S(2)}, u32[]{:S(2)}) collective-permute-start(f32[4,256,128]{2,1,0:T(8,128)} %own.1), channel_id=1, source_target_pairs={{0,8},{8,16},{16,24},{1,9},{9,17},{17,25},{2,10},{10,18},{18,26},{... | collective-permute-start | bytes 1572872 | tf_op jit(solution)/shard_map/ppermute | solution.py:171
  4.4 22.9 %collective-permute-start.2 = (f32[4,256,128]{2,1,0:T(8,128)}, f32[4,256,128]{2,1,0:T(8,128)S(1)}, u32[]{:S(2)}, u32[]{:S(2)}) collective-permute-start(f32[4,256,128]{2,1,0:T(8,128)} %own.1), channel_id=1, source_target_pairs={{0,4},{1,5},{2,6},{3,7},{4,0},{5,1},{6,2},{7,3},{24,28},{25,29},{2... | collective-permute-start | bytes 1572872 | tf_op jit(solution)/shard_map/ppermute | solution.py:170
  10.4 16.2 %copy-start.5 = (s32[4]{0:T(128)}, s32[4]{0:T(128)S(1)}, u32[]{:S(2)}) copy-start(s32[4]{0:T(128)S(1)} %broadcast_select_fusion.4.order_ref) | copy-start | bytes 52
  27.2 0.8 %copy-start = (f32[4,256,128]{2,1,0:T(8,128)}, f32[4,256,128]{2,1,0:T(8,128)S(1)}, u32[]{:S(2)}) copy-start(f32[4,256,128]{2,1,0:T(8,128)S(1)} %collective-permute-done.1.below) | copy-start | bytes 1572868
  27.2 1.0 %copy-start.1 = (f32[4,256,128]{2,1,0:T(8,128)}, f32[4,256,128]{2,1,0:T(8,128)S(1)}, u32[]{:S(2)}) copy-start(f32[4,256,128]{2,1,0:T(8,128)S(1)} %collective-permute-done.above) | copy-start | bytes 1572868
  27.2 1.1 %copy-start.2 = (f32[4,256,128]{2,1,0:T(8,128)}, f32[4,256,128]{2,1,0:T(8,128)S(1)}, u32[]{:S(2)}) copy-start(f32[4,256,128]{2,1,0:T(8,128)S(1)} %collective-permute-done.2.turned) | copy-start | bytes 1572868
  40.6 15.9 %collective-permute-start.3 = (f32[192,256]{1,0:T(8,128)}, f32[192,256]{1,0:T(8,128)S(1)}, u32[]{:S(2)}, u32[]{:S(2)}) collective-permute-start(f32[192,256]{1,0:T(8,128)} %get-tuple-element.25), channel_id=1, source_target_pairs={{0,7},{1,0},{2,1},{3,2},{4,3},{5,4},{6,5},{7,6},{8,15},{9,8},{10,9... | collective-permute-start | bytes 589832 | tf_op jit(solution)/shard_map/ppermute | solution.py:20
  42.9 13.6 %collective-permute-start.4 = (f32[192,256]{1,0:T(8,128)}, f32[192,256]{1,0:T(8,128)S(1)}, u32[]{:S(2)}, u32[]{:S(2)}) collective-permute-start(f32[192,256]{1,0:T(8,128)} %get-tuple-element.26), channel_id=1, source_target_pairs={{0,1},{1,2},{2,3},{3,4},{4,5},{5,6},{6,7},{7,0},{8,9},{9,10},{10,1... | collective-permute-start | bytes 589832 | tf_op jit(solution)/shard_map/ppermute | solution.py:20
  56.5 0.7 %copy-start.3 = (f32[192,256]{1,0:T(8,128)}, f32[192,256]{1,0:T(8,128)S(1)}, u32[]{:S(2)}) copy-start(f32[192,256]{1,0:T(8,128)S(1)} %collective-permute-done.3.east_ref) | copy-start | bytes 589828
  56.5 0.8 %copy-start.4 = (f32[192,256]{1,0:T(8,128)}, f32[192,256]{1,0:T(8,128)S(1)}, u32[]{:S(2)}) copy-start(f32[192,256]{1,0:T(8,128)S(1)} %collective-permute-done.4.west_ref) | copy-start | bytes 589828
